TPU v7x, 128 devices: a whole 4x4x4 slice. The times are simulated.
128 devices in a mesh: ctx: 32 (over x, y_hi, z), head: 4 (over y_lo, core).
Axes of the slice: x: 4, y: 4 (y_hi: 2, y_lo: 2; y = y_hi * 2 + y_lo), z: 4, core: 2. Of those that a mesh axis runs over, the one named last changes fastest.
Arguments:
- queries: bfloat16 [4096, 4096], P('ctx', 'head'), may hold values from -6 to 6
- keys_new: bfloat16 [4096, 1024], P('ctx', 'head'), may hold values from -6 to 6
- values_new: bfloat16 [4096, 1024], P('ctx', 'head'), may hold values from -6 to 6
- cache_keys: bfloat16 [32768, 1024], P('ctx', 'head'), may hold values from -6 to 6
- cache_values: bfloat16 [32768, 1024], P('ctx', 'head'), may hold values from -6 to 6
- block_list: int32 [8, 32, 64], P('head', 'ctx'), may hold values from -1 to 255, as said below
- block_count: int32 [8, 32], P('head', 'ctx'), may hold values from 0 to 64
- out_weight: bfloat16 [4096, 4096], P('head'), may hold values from -0.21875 to 0.21875
Outputs:
- mixed: bfloat16 [4096, 4096], P(('ctx', 'head'))
Inputs may be any that keep to these rules, and one draw needn't show every extreme that they name: `block_list`: row (h, q) holds distinct cache block numbers in increasing order in its first block_count[h, q] entries and -1 after them. For each KV head, the query blocks of one aligned run of 1 query block together list at most 2 blocks of each aligned run of 8 cache blocks and at least one; for every KV head some run lists exactly 2 of every run of cache blocks.
All inputs are finite; a program needn't handle non-finite values.
Results may differ from a plain program's by a relative error of at most 0.015.
Values may be sent and summed in bfloat16 or wider, within the bound.
No kernel may reach another device: no remote copies, remote signals or barrier semaphores. Data moves between devices by JAX's collectives and lax.ppermute only.
A program may use at most 192 MiB of HBM per device.

v0:
```python
import jax
import jax.numpy as jnp
from jax import lax
from jax.sharding import PartitionSpec as P

HD = 128
BLOCK = 128
CAP = 2
CB_DEV = 8


def passed_along(shard, axis, by):
    devices = lax.axis_size(axis)
    pairs = [(i, i + by) for i in range(devices) if 0 <= i + by < devices]
    return lax.ppermute(shard, axis, pairs)


def wanted(block_rows, counts, block_ids):
    in_use = jnp.arange(block_rows.shape[2])[None, None, :] < counts[:, :, None]
    matches = (block_rows[:, :, :, None] == block_ids[None, None, None, :]) & in_use[:, :, :, None]
    return jnp.any(matches, axis=2)


def slot_table(union_mask):
    position = jnp.cumsum(union_mask.astype(jnp.int32), axis=-1) - 1
    return union_mask[:, :, None, :] & (
        position[:, :, None, :] == jnp.arange(CAP)[None, None, :, None]
    )


def shards(
    queries, keys_new, values_new, cache_keys, cache_values, block_list, block_count, out_weight
):
    n_ctx = lax.axis_size("ctx")
    my_index = lax.axis_index("ctx")
    kv_local = keys_new.shape[1] // HD
    group_size = queries.shape[1] // keys_new.shape[1]
    row_count = queries.shape[0]
    qb_dev = row_count // BLOCK
    nblocks = n_ctx * CB_DEV
    slot_count = n_ctx * CAP
    per_query = wanted(block_list, block_count, jnp.arange(nblocks, dtype=jnp.int32))
    union_mask = jnp.any(per_query, axis=1).reshape(kv_local, n_ctx, CB_DEV)
    picker = slot_table(union_mask)
    per_owner = per_query.reshape(kv_local, qb_dev, n_ctx, CB_DEV)
    listed = jnp.any(picker[:, None] & per_owner[:, :, :, None, :], axis=-1).reshape(
        kv_local, qb_dev, slot_count
    )
    same_owner = jnp.arange(n_ctx)[:, None] == jnp.arange(n_ctx)[None, :]
    pick_global = (
        (picker[:, :, :, None, :] & same_owner[None, :, None, :, None])
        .reshape(kv_local, slot_count, nblocks)
        .astype(jnp.bfloat16)
    )
    pieces = (
        lax.all_gather(cache_keys, "ctx", axis=0, tiled=True),
        lax.all_gather(cache_values, "ctx", axis=0, tiled=True),
    )
    piece_blocks = pieces[0].shape[0] // BLOCK
    piece_keys = pieces[0].reshape(piece_blocks, BLOCK, kv_local, HD)
    piece_values = pieces[1].reshape(piece_blocks, BLOCK, kv_local, HD)
    keys_part = jnp.einsum(
        "hsb,bthd->hstd", pick_global, piece_keys, preferred_element_type=jnp.float32
    ).astype(jnp.bfloat16)
    values_part = jnp.einsum(
        "hsb,bthd->hstd", pick_global, piece_values, preferred_element_type=jnp.float32
    ).astype(jnp.bfloat16)
    prev_keys, prev_values = passed_along((keys_new, values_new), "ctx", 1)
    stretch_keys = jnp.concatenate([prev_keys, keys_new], axis=0)
    stretch_values = jnp.concatenate([prev_values, values_new], axis=0)
    row_ids = jnp.arange(row_count)[:, None]
    key_ids = jnp.arange(BLOCK + row_count)[None, :] - BLOCK
    stretch_ok = (
        (key_ids <= row_ids)
        & (key_ids >= (row_ids // BLOCK - 1) * BLOCK)
        & ((my_index > 0) | (key_ids >= 0))
    )
    score_scale = HD ** (-0.5)
    head_outputs = []
    for kv_head in range(kv_local):
        cache_keyhead = keys_part[kv_head].reshape(slot_count * BLOCK, HD)
        cache_valuehead = values_part[kv_head].reshape(slot_count * BLOCK, HD)
        stretch_keyhead = stretch_keys[:, kv_head * HD : (kv_head + 1) * HD]
        stretch_valuehead = stretch_values[:, kv_head * HD : (kv_head + 1) * HD]
        block_ok = listed[kv_head]
        for member in range(group_size):
            column = (kv_head * group_size + member) * HD
            query_head = queries[:, column : column + HD]
            cache_scores = (
                jnp.einsum(
                    "rd,kd->rk", query_head, cache_keyhead, preferred_element_type=jnp.float32
                )
                * score_scale
            )
            cache_scores = jnp.where(
                block_ok[:, None, :, None],
                cache_scores.reshape(qb_dev, BLOCK, slot_count, BLOCK),
                -jnp.inf,
            ).reshape(row_count, slot_count * BLOCK)
            stretch_scores = (
                jnp.einsum(
                    "rd,kd->rk", query_head, stretch_keyhead, preferred_element_type=jnp.float32
                )
                * score_scale
            )
            stretch_scores = jnp.where(stretch_ok, stretch_scores, -jnp.inf)
            row_max = jnp.maximum(jnp.max(cache_scores, axis=1), jnp.max(stretch_scores, axis=1))[
                :, None
            ]
            cache_weights = jnp.exp(cache_scores - row_max)
            stretch_weights = jnp.exp(stretch_scores - row_max)
            weight_sum = jnp.sum(cache_weights, axis=1) + jnp.sum(stretch_weights, axis=1)
            mixture = jnp.dot(
                cache_weights.astype(jnp.bfloat16),
                cache_valuehead,
                preferred_element_type=jnp.float32,
            )
            mixture = mixture + jnp.dot(
                stretch_weights.astype(jnp.bfloat16),
                stretch_valuehead,
                preferred_element_type=jnp.float32,
            )
            head_outputs.append((mixture / weight_sum[:, None]).astype(jnp.bfloat16))
    attention = jnp.concatenate(head_outputs, axis=1)
    mixed = lax.psum_scatter(
        jnp.dot(attention, out_weight, preferred_element_type=jnp.float32).astype(jnp.bfloat16),
        "head",
        scatter_dimension=0,
        tiled=True,
    )
    return mixed


def solution(mesh):
    return jax.shard_map(
        shards,
        mesh=mesh,
        in_specs=(
            P("ctx", "head"),
            P("ctx", "head"),
            P("ctx", "head"),
            P("ctx", "head"),
            P("ctx", "head"),
            P("head", "ctx", None),
            P("head", "ctx"),
            P("head", None),
        ),
        out_specs=P(("ctx", "head"), None),
        check_vma=False,
    )
```

profile of v0, /device:TPU:1, one launch (start us, length us, event | category | flops | bytes accessed | tf_op | source)
XLA Modules:
  0.0 437.3 jit_solution(14608742840540978373)
XLA Ops:
  8.1 4.4 %collective-permute-start = (bf16[128,256]{1,0:T(8,128)(2,1)}, bf16[128,256]{1,0:T(8,128)(2,1)S(1)}, u32[]{:S(2)}, u32[]{:S(2)}) collective-permute-start(bf16[128,256]{1,0:T(8,128)(2,1)} %param.9), channel_id=1, source_target_pairs={{0,4},{4,8},{8,12},{12,16},{16,20},{20,24},{24,28},{28,32},{32,36}... | collective-permute-start | bytes 196616 | tf_op jit(solution)/shard_map/ppermute | solution.py:15
  12.4 3.5 collective-permute-start.1
  18.3 1.3 and.111
  26.1 142.4 %all-gather.3.cloned.1.call-done = bf16[32768,256]{1,0:T(8,128)(2,1)} async-done(((bf16[1024,256]{1,0:T(8,128)(2,1)}), bf16[32768,256]{1,0:T(8,128)(2,1)}) %all-gather.3.cloned.1.call-update) | async-done | bytes 16777232 | tf_op jit(solution)/shard_map/all_gather | solution.py:56
  168.5 24.3 %reshape.304 = bf16[256,128,2,128]{3,2,1,0:T(2,128)(2,1)} reshape(bf16[32768,256]{1,0:T(8,128)(2,1)} %all-gather.3.cloned.1.call-done) | data formatting | bytes 33554432 | tf_op jit(solution)/shard_map/reshape | solution.py:60
  192.8 24.9 %fusion.28 = bf16[2,64,128,128]{3,1,2,0:T(8,128)(2,1)S(1)} fusion(bf16[256,128,2,128]{3,2,1,0:T(2,128)(2,1)} %reshape.304, pred[2,64,256]{2,1,0:T(32,128)(4,1)S(1)} %and.111, pred[64,256]{1,0:T(8,128)(4,1)S(1)} %and.113), kind=kOutput, calls=%fused_computation.45 | convolution fusion | flops 1075871744 | bytes 21020672 | tf_op jit(solution)/shard_map/hsb,bthd->hstd/dot_general | solution.py:62
  217.7 2.3 fusion.177
  220.0 1.4 copy.22
  221.4 5.6 %fusion.180 = (f32[128]{0:T(128)S(1)}, f32[8192,128]{1,0:T(8,128)}) fusion(bf16[8192,128]{1,0:T(8,128)(2,1)S(1)} %bitcast.71, bf16[128,1024]{1,0:T(8,128)(2,1)S(1)} %copy-done.3, pred[8192]{0:T(1024)(128)(4,1)S(1)} %broadcast_bitcast_fusion.1), kind=kOutput, calls=%fused_computation.220 | convolution fusion | flops 271581056 | bytes 6332928 | tf_op jit(solution)/shard_map/rd,kd->rk/dot_general | solution.py:90
  227.0 5.6 %fusion.182 = (f32[128]{0:T(128)S(1)}, f32[8192,128]{1,0:T(8,128)}) fusion(bf16[8192,128]{1,0:T(8,128)(2,1)S(1)} %bitcast.72, bf16[128,1024]{1,0:T(8,128)(2,1)S(1)} %copy-done.3, pred[8192]{0:T(1024)(128)(4,1)S(1)} %broadcast_bitcast_fusion.1), kind=kOutput, calls=%fused_computation.222 | convolution fusion | flops 271581056 | bytes 6332928 | tf_op jit(solution)/shard_map/rd,kd->rk/dot_general | solution.py:90
  232.5 92.0 %all-gather.5.cloned.1.call-done = bf16[32768,256]{1,0:T(8,128)(2,1)} async-done(((bf16[1024,256]{1,0:T(8,128)(2,1)}), bf16[32768,256]{1,0:T(8,128)(2,1)}) %all-gather.5.cloned.1.call-update) | async-done | bytes 16777232 | tf_op jit(solution)/shard_map/all_gather | solution.py:57
  324.6 23.9 %reshape.305 = bf16[256,128,2,128]{3,2,1,0:T(2,128)(2,1)} reshape(bf16[32768,256]{1,0:T(8,128)(2,1)} %all-gather.5.cloned.1.call-done) | data formatting | bytes 33554432 | tf_op jit(solution)/shard_map/reshape | solution.py:61
  348.5 25.0 %fusion.31 = bf16[2,64,128,128]{3,1,2,0:T(8,128)(2,1)S(1)} fusion(bf16[256,128,2,128]{3,2,1,0:T(2,128)(2,1)} %reshape.305, pred[2,64,256]{2,1,0:T(32,128)(4,1)S(1)} %and.111, pred[64,256]{1,0:T(8,128)(4,1)S(1)} %and.113), kind=kOutput, calls=%fused_computation.46 | convolution fusion | flops 1075871744 | bytes 21020672 | tf_op jit(solution)/shard_map/hsb,bthd->hstd/dot_general | solution.py:65
  374.5 1.4 copy.25
  377.8 1.2 fusion.48
  380.0 1.3 fusion.46
  382.4 1.3 fusion.184
  383.7 1.2 fusion.44
  385.9 1.3 fusion.186
  387.2 1.2 fusion.42
  389.5 1.4 copy.27
  390.8 1.3 fusion.188
  392.1 1.5 fusion.190
  393.6 1.4 copy.28
  396.1 1.2 fusion.40
  397.3 1.2 fusion.38
  399.5 1.3 fusion.192
  400.8 1.2 fusion.36
  403.1 1.3 fusion.194
  404.4 1.4 fusion.34
  409.4 2.3 convolution_convert_fusion
  411.7 18.8 %reduce-scatter.2.cloned.1.call-done = bf16[32,4096]{1,0:T(8,128)(2,1)} async-done(((bf16[128,4096]{1,0:T(8,128)(2,1)}), bf16[32,4096]{1,0:T(8,128)(2,1)}) %reduce-scatter.2.cloned.1.call-update) | async-done | bytes 262160 | tf_op jit(solution)/shard_map/reduce_scatter | solution.py:125
  (102 shorter events, 24.3 us)
Async XLA Ops:
  6.5 18.3 %copy-start.3 = (bf16[128,1024]{1,0:T(8,128)(2,1)S(1)}, bf16[128,1024]{1,0:T(8,128)(2,1)}, u32[]{:S(2)}) copy-start(bf16[128,1024]{1,0:T(8,128)(2,1)} %param.8) | copy-start | bytes 786436
  6.5 162.0 %all-gather.3.cloned.1.call-start = ((), (), s32[]{:S(2)}) async-start(), calls=%async_computation.1 | async-start | bytes 17301504 | tf_op jit(solution)/shard_map/all_gather | solution.py:56
  7.3 317.3 %all-gather.5.cloned.1.call-start = ((), (), s32[]{:S(2)}) async-start(), calls=%async_computation.2 | async-start | bytes 17301504 | tf_op jit(solution)/shard_map/all_gather | solution.py:57
  8.0 422.5 %reduce-scatter.2.cloned.1.call-start = ((), (), s32[]{:S(2)}) async-start(), calls=%async_computation.3 | async-start | bytes 1310720 | tf_op jit(solution)/shard_map/reduce_scatter | solution.py:125
  8.1 13.1 %collective-permute-start = (bf16[128,256]{1,0:T(8,128)(2,1)}, bf16[128,256]{1,0:T(8,128)(2,1)S(1)}, u32[]{:S(2)}, u32[]{:S(2)}) collective-permute-start(bf16[128,256]{1,0:T(8,128)(2,1)} %param.9), channel_id=1, source_target_pairs={{0,4},{4,8},{8,12},{12,16},{16,20},{20,24},{24,28},{28,32},{32,36}... | collective-permute-start | bytes 196616 | tf_op jit(solution)/shard_map/ppermute | solution.py:15
  12.4 9.6 %collective-permute-start.1 = (bf16[128,256]{1,0:T(8,128)(2,1)}, bf16[128,256]{1,0:T(8,128)(2,1)S(1)}, u32[]{:S(2)}, u32[]{:S(2)}) collective-permute-start(bf16[128,256]{1,0:T(8,128)(2,1)} %param.10), channel_id=1, source_target_pairs={{0,4},{4,8},{8,12},{12,16},{16,20},{20,24},{24,28},{28,32},{32,36}... | collective-permute-start | bytes 196616 | tf_op jit(solution)/shard_map/ppermute | solution.py:15
  22.9 169.9 %copy-start.4 = (bf16[256,256]{1,0:T(8,128)(2,1)}, bf16[256,256]{1,0:T(8,128)(2,1)S(1)}, u32[]{:S(2)}) copy-start(bf16[256,256]{1,0:T(8,128)(2,1)S(1)} %constant_dynamic-update-slice_fusion.2) | copy-start | bytes 393220
  374.5 2.2 copy-start.1
  377.8 2.2 copy-start
  387.2 2.3 copy-start.2
  403.1 6.3 %slice-start = ((s8[8388608]{0:T(1024)(128)(4,1)}), s8[4194304]{0:T(1024)(128)(4,1)S(1)}, s32[]{:S(2)}) async-start(s8[8388608]{0:T(1024)(128)(4,1)} %bitcast.87), calls=%async_computation.4 | async-start | bytes 8388608
  404.4 5.0 %slice-start.1 = ((s8[8388608]{0:T(1024)(128)(4,1)}), s8[4194304]{0:T(1024)(128)(4,1)S(1)}, s32[]{:S(2)}) async-start(s8[8388608]{0:T(1024)(128)(4,1)} %bitcast.87), calls=%async_computation.5 | async-start | bytes 8388608
  405.8 1.7 copy-start.5
Sparse Core Ops, SparseCore 0:
  10.5 157.9 all-gather.2
  171.7 152.8 all-gather.4
  411.9 18.6 reduce-scatter.1
where the time goes:
time: 443 us; the launch traced here: 437 us
  waiting for transfers between devices  255 us (58%)
  matrix products  86 us (19%)
  local copies, waits for them, and re-layouts  63.5 us (14%)
  between operations  13.8 us (3%)
  other arithmetic  11.3 us (3%)
  starting transfers between devices  8 us (2%)
    all_gather x1, waiting for transfers between devices, shards(): lax.all_gather(cache_keys, 'ctx', axis=0, tiled=True)  142 us
    all_gather x1, waiting for transfers between devices, shards(): lax.all_gather(cache_values, 'ctx', axis=0, tiled=True)  92 us
    dot_general x1, matrix products, shards(): jnp.einsum('hsb,bthd->hstd', pick_global, piece_values, preferred_element...  25 us
    dot_general x1, matrix products, shards(): jnp.einsum('hsb,bthd->hstd', pick_global, piece_keys, preferred_element_t...  24.9 us
    reshape x1, local copies, waits for them, and re-layouts, shards(): piece_keys = pieces[0].reshape(piece_blocks, BLOCK, kv_local, HD)  24.3 us
    reshape x1, local copies, waits for them, and re-layouts, shards(): piece_values = pieces[1].reshape(piece_blocks, BLOCK, kv_local, HD)  23.9 us
    dot_general x8, matrix products, shards(): jnp.einsum('rd,kd->rk', query_head, cache_keyhead, preferred_element_type...  19 us
    reduce_scatter x1, waiting for transfers between devices, shards(): lax.psum_scatter(jnp.dot(attention, out_weight, preferred_element_type=jn...  18.8 us
  transfers between devices with their start and end apart: 5, of which 3 were waited for; matrix products, arithmetic and copies ran while one was open for 17% of the time, Pallas kernels for 0%

commit v1 on v0

--- a/solution.py
+++ b/solution.py
@@ -54,7 +54,9 @@
     )
     pieces = (
         lax.all_gather(cache_keys, "ctx", axis=0, tiled=True),
-        lax.all_gather(cache_values, "ctx", axis=0, tiled=True),
+        jnp.concatenate(
+            lax.all_to_all(jnp.stack([cache_values] * lax.axis_size("ctx")), "ctx", 0, 0), axis=0
+        ),
     )
     piece_blocks = pieces[0].shape[0] // BLOCK
     piece_keys = pieces[0].reshape(piece_blocks, BLOCK, kv_local, HD)

time: 443 us -> 606 us (1.37)
  waiting for transfers between devices: 255 us -> 384 us
  local copies, waits for them, and re-layouts: 63.5 us -> 113 us
  matrix products: 86 us -> 59 us
  starting transfers between devices: 8 us -> 17.8 us
    all_to_all x0 -> x1, waiting for transfers between devices: none -> 184 us  [shards(): lax.all_to_all(jnp.stack([cache_values] * lax.axis_size('ctx')), 'ctx', 0...]
    ppermute x2, waiting for transfers between devices: 0.01 us -> 143 us  [passed_along(): return lax.ppermute(shard, axis, pairs)]
    all_gather x1, waiting for transfers between devices: 142 us -> 0.02 us  [shards(): lax.all_gather(cache_keys, 'ctx', axis=0, tiled=True)]
    all_gather x1 -> x0, waiting for transfers between devices: 92 us -> none  [shards(): lax.all_gather(cache_values, 'ctx', axis=0, tiled=True)]
    another operation x0 -> x3, local copies, waits for them, and re-layouts: none -> 56 us  [the longest x2 50 us: shards(): piece_values = pieces[1].reshape(piece_blocks, BLOCK, kv_local, HD)]
    reduce_scatter x1, waiting for transfers between devices: 18.8 us -> 56.5 us  [shards(): lax.psum_scatter(jnp.dot(attention, out_weight, preferred_element_type=jn...]
    reshape x1 -> x0, local copies, waits for them, and re-layouts: 23.9 us -> none  [shards(): piece_values = pieces[1].reshape(piece_blocks, BLOCK, kv_local, HD)]
    all_to_all x0 -> x1, local copies, waits for them, and re-layouts: none -> 18.8 us  [shards(): lax.all_to_all(jnp.stack([cache_values] * lax.axis_size('ctx')), 'ctx', 0...]
  transfers between devices with their start and end apart: 5 -> 5, of which waited for: 3 -> 4; matrix products, arithmetic and copies ran while one was open for 17% -> 16% of each run, Pallas kernels for 0% -> 0%
where the time goes in v1:
time: 606 us; the launch traced here: 598 us
  waiting for transfers between devices  384 us (63%)
  local copies, waits for them, and re-layouts  113 us (19%)
  matrix products  59 us (10%)
  starting transfers between devices  17.8 us (3%)
  between operations  14.1 us (2%)
  other arithmetic  10.2 us (2%)
    all_to_all x1, waiting for transfers between devices, shards(): lax.all_to_all(jnp.stack([cache_values] * lax.axis_size('ctx')), 'ctx', 0...  184 us
    ppermute x2, waiting for transfers between devices, passed_along(): return lax.ppermute(shard, axis, pairs)  143 us
    reduce_scatter x1, waiting for transfers between devices, shards(): lax.psum_scatter(jnp.dot(attention, out_weight, preferred_element_type=jn...  56.5 us
    another operation x2, local copies, waits for them, and re-layouts, shards(): piece_values = pieces[1].reshape(piece_blocks, BLOCK, kv_local, HD)  50 us
    dot_general x1, matrix products, shards(): jnp.einsum('hsb,bthd->hstd', pick_global, piece_keys, preferred_element_t...  24.8 us
    reshape x1, local copies, waits for them, and re-layouts, shards(): piece_keys = pieces[0].reshape(piece_blocks, BLOCK, kv_local, HD)  24.2 us
    all_to_all x1, local copies, waits for them, and re-layouts, shards(): lax.all_to_all(jnp.stack([cache_values] * lax.axis_size('ctx')), 'ctx', 0...  18.8 us
  transfers between devices with their start and end apart: 5, of which 4 were waited for; matrix products, arithmetic and copies ran while one was open for 16% of the time, Pallas kernels for 0%

profile of v1, /device:TPU:1, one launch (start us, length us, event | category | flops | bytes accessed | tf_op | source)
XLA Modules:
  0.0 598.0 jit_solution(924320827280614133)
XLA Ops:
  7.3 1.2 copy.32
  8.5 6.0 stack.2
  14.5 11.6 %all-to-all-start = ((bf16[32,1024,256]{1,2,0:T(8,128)(2,1)}), bf16[32,1024,256]{1,2,0:T(8,128)(2,1)}, u32[]{:S(2)}, u32[]{:S(2)}) async-start(bf16[32,1024,256]{1,2,0:T(8,128)(2,1)} %stack.2), calls=%async_computation | async-start | bytes 33554432 | tf_op jit(solution)/shard_map/all_to_all | solution.py:58
  26.2 3.1 collective-permute-start
  29.3 3.1 collective-permute-start.1
  33.4 1.3 and.111
  36.2 141.5 %collective-permute-done = bf16[128,256]{1,0:T(8,128)(2,1)S(1)} collective-permute-done((bf16[128,256]{1,0:T(8,128)(2,1)S(1)}, bf16[128,256]{1,0:T(8,128)(2,1)S(1)}, u32[]{:S(2)}, u32[]{:S(2)}) %collective-permute-start) | collective-permute-done | bytes 65568 | tf_op jit(solution)/shard_map/ppermute | solution.py:15
  177.8 1.5 collective-permute-done.1
  181.0 183.9 %all-to-all-done = bf16[32,1024,256]{1,2,0:T(8,128)(2,1)} async-done(((bf16[32,1024,256]{1,2,0:T(8,128)(2,1)}), bf16[32,1024,256]{1,2,0:T(8,128)(2,1)}, u32[]{:S(2)}, u32[]{:S(2)}) %all-to-all-start) | async-done | bytes 16777248 | tf_op jit(solution)/shard_map/all_to_all | solution.py:58
  364.9 18.8 %copy.33 = bf16[32,1024,256]{1,0,2:T(8,128)(2,1)} copy(bf16[32,1024,256]{1,2,0:T(8,128)(2,1)} %all-to-all-done) | data formatting | bytes 33554432 | tf_op jit(solution)/shard_map/all_to_all | solution.py:58
  383.7 25.5 %reshape_reshape.3 = bf16[256,128,2,128]{1,0,3,2:T(8,128)(2,1)} reshape(bf16[32,1024,256]{1,0,2:T(8,128)(2,1)} %copy.33) | data formatting | bytes 33554432 | tf_op jit(solution)/shard_map/reshape;reshape | solution.py:63
  409.2 24.5 %copy.34 = bf16[256,128,2,128]{3,0,1,2:T(8,128)(2,1)} copy(bf16[256,128,2,128]{1,0,3,2:T(8,128)(2,1)} %reshape_reshape.3) | data formatting | bytes 33554432 | tf_op jit(solution)/shard_map/reshape;reshape | solution.py:63
  433.8 8.8 %convolution_convert_fusion.1 = bf16[2,64,128,128]{3,1,2,0:T(8,128)(2,1)S(1)} fusion(bf16[256,128,2,128]{3,0,1,2:T(8,128)(2,1)} %copy.34, pred[2,64,256]{2,1,0:T(32,128)(4,1)S(1)} %and.111, pred[64,256]{1,0:T(8,128)(4,1)S(1)} %and.113), kind=kOutput, calls=%fused_computation.44 | convolution fusion | flops 1075871744 | bytes 21020672 | tf_op jit(solution)/shard_map/hsb,bthd->hstd/dot_general | solution.py:67
  443.5 2.7 copy.35
  446.2 1.4 copy.38
  447.5 24.2 %reshape.302 = bf16[256,128,2,128]{3,2,1,0:T(2,128)(2,1)} reshape(bf16[32768,256]{1,0:T(8,128)(2,1)} %all-gather.2.cloned.1.call-done) | data formatting | bytes 33554432 | tf_op jit(solution)/shard_map/reshape | solution.py:62
  471.7 24.8 %fusion.26 = bf16[2,64,128,128]{3,1,2,0:T(8,128)(2,1)S(1)} fusion(bf16[256,128,2,128]{3,2,1,0:T(2,128)(2,1)} %reshape.302, pred[2,64,256]{2,1,0:T(32,128)(4,1)S(1)} %and.111, pred[64,256]{1,0:T(8,128)(4,1)S(1)} %and.113), kind=kOutput, calls=%fused_computation.43 | convolution fusion | flops 1075871744 | bytes 21020672 | tf_op jit(solution)/shard_map/hsb,bthd->hstd/dot_general | solution.py:64
  497.5 1.4 copy.31
  498.9 1.3 fusion.175
  500.1 1.3 fusion.177
  501.4 1.3 fusion.10
  506.4 1.3 fusion.179
  510.0 1.3 fusion.181
  513.5 1.8 copy.37
  515.3 1.3 fusion.183
  516.5 1.3 fusion.185
  518.9 1.2 fusion.35
  522.4 1.3 fusion.187
  525.9 1.3 fusion.189
  527.2 1.3 fusion.29
  532.2 2.3 convolution_convert_fusion
  534.5 56.5 %reduce-scatter.2.cloned.1.call-done = bf16[32,4096]{1,0:T(8,128)(2,1)} async-done(((bf16[128,4096]{1,0:T(8,128)(2,1)}), bf16[32,4096]{1,0:T(8,128)(2,1)}) %reduce-scatter.2.cloned.1.call-update) | async-done | bytes 262160 | tf_op jit(solution)/shard_map/reduce_scatter | solution.py:127
  (109 shorter events, 24.3 us)
Async XLA Ops:
  6.5 441.0 %all-gather.2.cloned.1.call-start = ((), (), s32[]{:S(2)}) async-start(), calls=%async_computation.2 | async-start | bytes 17301504 | tf_op jit(solution)/shard_map/all_gather | solution.py:56
  14.5 11.7 %copy-start.2 = (bf16[128,256]{1,0:T(8,128)(2,1)S(1)}, bf16[128,256]{1,0:T(8,128)(2,1)}, u32[]{:S(2)}) copy-start(bf16[128,256]{1,0:T(8,128)(2,1)} %param.9) | copy-start | bytes 196612
  14.5 14.8 %copy-start.3 = (bf16[128,256]{1,0:T(8,128)(2,1)S(1)}, bf16[128,256]{1,0:T(8,128)(2,1)}, u32[]{:S(2)}) copy-start(bf16[128,256]{1,0:T(8,128)(2,1)} %param.10) | copy-start | bytes 196612
  14.5 17.9 %copy-start.7 = (s32[2,1]{0,1:T(1,128)S(1)}, s32[2,1]{0,1:T(1,128)}, u32[]{:S(2)}) copy-start(s32[2,1]{0,1:T(1,128)} %param.14) | copy-start | bytes 28
  14.5 18.0 %copy-start.6 = (s32[2,1,64]{2,1,0:T(1,128)S(1)}, s32[2,1,64]{2,1,0:T(1,128)}, u32[]{:S(2)}) copy-start(s32[2,1,64]{2,1,0:T(1,128)} %param.13) | copy-start | bytes 1540
  14.5 164.8 %copy-start.1 = (bf16[128,1024]{1,0:T(8,128)(2,1)S(1)}, bf16[128,1024]{1,0:T(8,128)(2,1)}, u32[]{:S(2)}) copy-start(bf16[128,1024]{1,0:T(8,128)(2,1)} %param.8) | copy-start | bytes 786436
  14.5 350.4 %all-to-all-start = ((bf16[32,1024,256]{1,2,0:T(8,128)(2,1)}), bf16[32,1024,256]{1,2,0:T(8,128)(2,1)}, u32[]{:S(2)}, u32[]{:S(2)}) async-start(bf16[32,1024,256]{1,2,0:T(8,128)(2,1)} %stack.2), calls=%async_computation | async-start | bytes 33554432 | tf_op jit(solution)/shard_map/all_to_all | solution.py:58
  26.1 564.9 %reduce-scatter.2.cloned.1.call-start = ((), (), s32[]{:S(2)}) async-start(), calls=%async_computation.3 | async-start | bytes 1310720 | tf_op jit(solution)/shard_map/reduce_scatter | solution.py:127
  26.2 151.6 %collective-permute-start = (bf16[128,256]{1,0:T(8,128)(2,1)S(1)}, bf16[128,256]{1,0:T(8,128)(2,1)S(1)}, u32[]{:S(2)}, u32[]{:S(2)}) collective-permute-start(bf16[128,256]{1,0:T(8,128)(2,1)S(1)} %copy-done.2), channel_id=1, source_target_pairs={{0,4},{4,8},{8,12},{12,16},{16,20},{20,24},{24,28},{28,32},{32,36}... | collective-permute-start | bytes 196616 | tf_op jit(solution)/shard_map/ppermute | solution.py:15
  29.3 150.0 %collective-permute-start.1 = (bf16[128,256]{1,0:T(8,128)(2,1)S(1)}, bf16[128,256]{1,0:T(8,128)(2,1)S(1)}, u32[]{:S(2)}, u32[]{:S(2)}) collective-permute-start(bf16[128,256]{1,0:T(8,128)(2,1)S(1)} %copy-done.3), channel_id=1, source_target_pairs={{0,4},{4,8},{8,12},{12,16},{16,20},{20,24},{24,28},{28,32},{32,36}... | collective-permute-start | bytes 196616 | tf_op jit(solution)/shard_map/ppermute | solution.py:15
  179.3 204.4 %copy-start.4 = (bf16[256,256]{1,0:T(8,128)(2,1)}, bf16[256,256]{1,0:T(8,128)(2,1)S(1)}, u32[]{:S(2)}) copy-start(bf16[256,256]{1,0:T(8,128)(2,1)S(1)} %constant_dynamic-update-slice_fusion.2) | copy-start | bytes 393220
  501.4 1.6 copy-start
  525.9 6.3 %slice-start = ((s8[8388608]{0:T(1024)(128)(4,1)}), s8[4194304]{0:T(1024)(128)(4,1)S(1)}, s32[]{:S(2)}) async-start(s8[8388608]{0:T(1024)(128)(4,1)} %bitcast.90), calls=%async_computation.4 | async-start | bytes 8388608
  527.2 5.0 slice-start.1
  528.6 1.7 copy-start.5
Sparse Core Ops, SparseCore 0:
  10.6 402.0 all-gather.1
  534.6 56.3 reduce-scatter.1
